TPU v7x, 256 devices: a whole 4x4x8 slice. The times are simulated.
256 devices in a mesh: seq: 64 (over z, y, core), head: 4 (over x).
Axes of the slice: x: 4, y: 4, z: 8, core: 2. Of those that a mesh axis runs over, the one named last changes fastest.
Arguments:
- hidden_in: bfloat16 [16384, 2048], P('seq', 'head'), may hold values from -6 to 6
- ple_in: bfloat16 [16384, 256], P('seq'), may hold values from -6 to 6
- group_map: int32 [128, 1], replicated, may hold values from 0 to 11
- prompt_len: int32 [12], replicated, may hold values from 1 to 8192, as said below
- cache: bfloat16 [12, 8192, 1024], P(None, 'seq', 'head'), may hold values from -6 to 6
- w_query: bfloat16 [2048, 2048], P(None, 'head'), may hold values from -0.125 to 0.125
- key_value_weight: bfloat16 [2048, 1024], P(None, 'head'), may hold values from -0.125 to 0.125
- w_out: bfloat16 [2048, 2048], P('head'), may hold values from -0.125 to 0.125
- in_gain: float32 [2048], replicated, may hold values from 0.5 to 2
- q_gain: float32 [256], replicated
- k_gain: float32 [256], replicated, may hold values from 0.5 to 2
- post_gain: float32 [2048], replicated, may hold values from 0.5 to 2
- laurel_left: bfloat16 [2048, 64], replicated, may hold values from -0.125 to 0.125
- laurel_right: bfloat16 [64, 2048], replicated, may hold values from -0.75 to 0.75
- laurel_gain: float32 [2048], replicated, may hold values from 0.5 to 2
- w_plgate: bfloat16 [2048, 256], replicated, may hold values from -0.125 to 0.125
- w_plproj: bfloat16 [256, 2048], replicated, may hold values from -0.375 to 0.375
- ple_gain: float32 [2048], replicated, may hold values from 0.5 to 2
Outputs:
- layer_out: bfloat16 [16384, 2048], P('seq', 'head')
Inputs may be any that keep to these rules, and one draw needn't show every extreme that they name: `group_map`: every one of the 12 groups is named by at least one request. `prompt_len`: some group's prompt fills all 8192 slots.
All inputs are finite; a program needn't handle non-finite values.
Results may differ from a plain program's by a relative error of at most 0.011.
The roundings to bfloat16 on the way count: a program that leaves them out, or rounds other values in their place, can miss the bound.
Values may be sent and summed in bfloat16 or wider, within the bound.
A program may use at most 128 MiB of HBM per device.

v0:
```python
import math

import jax
import jax.numpy as jnp
from jax import lax
from jax.sharding import PartitionSpec as P

NEW = 128


epsilon = 1e-06
theta_base = 1000000.0


def partner(value, axis, stride):
    mask = 2**stride
    pairs = [(source, source ^ mask) for source in range(lax.axis_size(axis))]
    return lax.ppermute(value, axis, pairs)


def norm_rows(values):
    return values * lax.rsqrt(jnp.mean(values * values, axis=-1, keepdims=True) + epsilon)


def rotate(values, positions):
    half_width = values.shape[-1] // 2
    inverse = theta_base ** (-jnp.arange(half_width, dtype=jnp.float32) / half_width)
    angles = positions.astype(jnp.float32)[:, None] * inverse[None, :]
    cosine = jnp.cos(angles)[:, None, :]
    sine_part = jnp.sin(angles)[:, None, :]
    front_half = values[..., :half_width]
    back_half = values[..., half_width:]
    return jnp.concatenate(
        [front_half * cosine - back_half * sine_part, back_half * cosine + front_half * sine_part],
        axis=-1,
    )


def contract_last(left_rows, right_rows):
    return lax.dot_general(
        left_rows, right_rows, (((1,), (1,)), ((), ())), preferred_element_type=jnp.float32
    )


def attend(queries, cached_keys, cached_values, new_keys, new_values, length):
    tokens, head_count, head_width = queries.shape
    query_rows = queries.reshape(tokens * head_count, head_width)
    cache_scores = contract_last(query_rows, cached_keys)
    fresh_scores = contract_last(query_rows, new_keys)
    valid_keys = jnp.arange(cached_keys.shape[0], dtype=jnp.int32) < length
    row_token = jnp.arange(tokens * head_count, dtype=jnp.int32) // head_count
    causal = jnp.arange(tokens, dtype=jnp.int32)[None, :] <= row_token[:, None]
    cache_scores = jnp.where(valid_keys[None, :], cache_scores, -1e30)
    fresh_scores = jnp.where(causal, fresh_scores, -1e30)
    highest = jnp.maximum(jnp.max(cache_scores, axis=1), jnp.max(fresh_scores, axis=1))
    cache_weights = jnp.exp(cache_scores - highest[:, None])
    fresh_weights = jnp.exp(fresh_scores - highest[:, None])
    totals = jnp.sum(cache_weights, axis=1) + jnp.sum(fresh_weights, axis=1)
    mixture = jnp.dot(
        cache_weights.astype(jnp.bfloat16), cached_values, preferred_element_type=jnp.float32
    )
    mixture = mixture + jnp.dot(
        fresh_weights.astype(jnp.bfloat16), new_values, preferred_element_type=jnp.float32
    )
    return (mixture / totals[:, None]).reshape(tokens, head_count, head_width).astype(jnp.bfloat16)


def finish(
    residual,
    normed_input,
    projected,
    ple_in,
    post_gain,
    laurel_left,
    laurel_right,
    laurel_gain,
    w_plgate,
    w_plproj,
    ple_gain,
):
    attn_branch = norm_rows(projected) * post_gain
    low_rank = jnp.dot(normed_input, laurel_left, preferred_element_type=jnp.float32).astype(
        jnp.bfloat16
    )
    laurel_out = jnp.dot(low_rank, laurel_right, preferred_element_type=jnp.float32)
    laurel_branch = normed_input.astype(jnp.float32) + norm_rows(laurel_out) * laurel_gain
    combined = (residual + attn_branch + laurel_branch) * math.sqrt(0.5)
    gate_in = jnp.dot(combined.astype(jnp.bfloat16), w_plgate, preferred_element_type=jnp.float32)
    gated = (jax.nn.gelu(gate_in, approximate=True) * ple_in.astype(jnp.float32)).astype(
        jnp.bfloat16
    )
    ple_out = jnp.dot(gated, w_plproj, preferred_element_type=jnp.float32)
    return (combined + norm_rows(ple_out) * ple_gain).astype(jnp.bfloat16)


def shards(
    hidden_in,
    ple_in,
    group_map,
    prompt_len,
    cache,
    w_query,
    key_value_weight,
    w_out,
    in_gain,
    q_gain,
    k_gain,
    post_gain,
    laurel_left,
    laurel_right,
    laurel_gain,
    w_plgate,
    w_plproj,
    ple_gain,
):
    seq_count = lax.axis_size("seq")
    seq_index = lax.axis_index("seq")
    head_index = lax.axis_index("head")
    head_width = q_gain.shape[0]
    tok_rows = hidden_in.shape[0]
    req_count = tok_rows // NEW
    gathered = lax.all_gather(hidden_in, "head", axis=1, tiled=True)
    residual = gathered.astype(jnp.float32)
    normed_input = (norm_rows(residual) * in_gain).astype(jnp.bfloat16)
    all_groups = group_map[:, 0]
    my_groups = lax.dynamic_slice_in_dim(all_groups, seq_index * req_count, req_count)
    matches = my_groups[:, None] == jnp.arange(prompt_len.shape[0], dtype=jnp.int32)[None, :]
    my_lengths = jnp.sum(jnp.where(matches, prompt_len[None, :], 0), axis=1)
    positions = (my_lengths[:, None] + jnp.arange(NEW, dtype=jnp.int32)[None, :]).reshape(-1)
    queries = jnp.dot(normed_input, w_query, preferred_element_type=jnp.float32).reshape(
        tok_rows, -1, head_width
    )
    queries = rotate(norm_rows(queries) * q_gain, positions).astype(jnp.bfloat16)
    fresh_projected = jnp.dot(normed_input, key_value_weight, preferred_element_type=jnp.float32)
    fresh_normed = norm_rows(fresh_projected)
    fresh_keys = rotate((fresh_normed * k_gain)[:, None, :], positions)[:, 0, :]
    holds_keys = head_index % 2 == 0
    own_fresh = jnp.where(holds_keys, fresh_keys, fresh_normed).astype(jnp.bfloat16)
    dest_groups = all_groups.reshape(seq_count, req_count)
    other_cache, other_fresh = partner((cache, own_fresh), "head", 0)
    key_block = jnp.where(holds_keys, cache, other_cache)
    value_block = jnp.where(holds_keys, other_cache, cache)
    paired = jnp.concatenate([key_block, value_block], axis=2)
    outgoing = jnp.take(paired, dest_groups, axis=0)
    arrived = lax.all_to_all(outgoing, "seq", split_axis=0, concat_axis=2, tiled=True)[0]
    cached_keys = arrived[:, :, :head_width]
    cached_values = arrived[:, :, head_width:]
    new_keys = jnp.where(holds_keys, own_fresh, other_fresh)
    new_values = jnp.where(holds_keys, other_fresh, own_fresh)
    outputs = []
    for request_item in range(req_count):
        first_row = request_item * NEW
        outputs.append(
            attend(
                queries[first_row : first_row + NEW],
                cached_keys[request_item],
                cached_values[request_item],
                new_keys[first_row : first_row + NEW],
                new_values[first_row : first_row + NEW],
                my_lengths[request_item],
            )
        )
    attended = jnp.concatenate(outputs, axis=0).reshape(tok_rows, -1)
    partial_out = jnp.dot(attended, w_out, preferred_element_type=jnp.float32)
    projected = lax.psum(partial_out.astype(jnp.bfloat16), "head").astype(jnp.float32)
    result = finish(
        residual,
        normed_input,
        projected,
        ple_in,
        post_gain,
        laurel_left,
        laurel_right,
        laurel_gain,
        w_plgate,
        w_plproj,
        ple_gain,
    )
    column_share = result.shape[1] // lax.axis_size("head")
    return lax.dynamic_slice_in_dim(result, head_index * column_share, column_share, 1)


def solution(mesh):
    placed = (
        P("seq", "head"),
        P("seq", None),
        P(),
        P(),
        P(None, "seq", "head"),
        P(None, "head"),
        P(None, "head"),
        P("head", None),
        P(),
        P(),
        P(),
        P(),
        P(),
        P(),
        P(),
        P(),
        P(),
        P(),
    )
    return jax.shard_map(
        shards, mesh=mesh, in_specs=placed, out_specs=P("seq", "head"), check_vma=False
    )
```

profile of v0, /device:TPU:1, one launch (start us, length us, event | category | flops | bytes accessed | tf_op | source)
XLA Modules:
  0.0 529.8 jit_solution(9346428660692215667)
XLA Ops:
  6.5 2.0 collective-permute-start
  8.6 0.8 reshape_squeeze.6
  9.5 0.5 broadcast.253
  10.0 1.3 reduce.5
  11.5 13.4 %collective-permute-done = bf16[12,128,256]{2,1,0:T(8,128)(2,1)S(1)} collective-permute-done((bf16[12,128,256]{2,1,0:T(8,128)(2,1)}, bf16[12,128,256]{2,1,0:T(8,128)(2,1)S(1)}, u32[]{:S(2)}, u32[]{:S(2)}) %collective-permute-start) | collective-permute-done | bytes 786464 | tf_op jit(solution)/shard_map/ppermute | solution.py:18
  24.9 1.2 broadcast_select_fusion.2
  26.1 1.3 pad_maximum_fusion
  27.4 9.6 %gather_fusion = bf16[128,128,512]{2,1,0:T(8,128)(2,1)} fusion(bf16[12,128,512]{2,1,0:T(8,128)(2,1)} %pad_maximum_fusion, s32[1024]{0:T(1024)S(1)} %pad_clamp_fusion), kind=kCustom, calls=%fused_computation | custom fusion | bytes 33554944 | tf_op jit(solution)/shard_map/jit(_take)/gather | solution.py:144
  37.1 14.2 %broadcast_select_fusion = bf16[64,2,128,512]{3,2,1,0:T(8,128)(2,1)} fusion(bf16[64,2,128,512]{3,2,1,0:T(8,128)(2,1)} %bitcast.50, pred[64,2]{1,0:T(8,128)(4,1)S(1)} %compare_and_fusion), kind=kLoop, calls=%fused_computation.1 | loop fusion | flops 8388608 | bytes 33554560 | tf_op jit(solution)/shard_map/jit(_take)/select_n | solution.py:144
  51.2 14.6 %all-to-all-start = ((bf16[64,2,128,512]{3,2,1,0:T(8,128)(2,1)}), bf16[64,2,128,512]{3,2,1,0:T(8,128)(2,1)}, u32[]{:S(2)}, u32[]{:S(2)}) async-start(bf16[64,2,128,512]{3,2,1,0:T(8,128)(2,1)} %broadcast_select_fusion), calls=%async_computation | async-start | bytes 33554432 | tf_op jit(solution)/shard_map/all_to_all | solution.py:145
  65.9 0.7 all-gather.2.cloned.1.call-update
  66.7 0.6 and_select_fusion
  67.5 0.6 fusion.86
  68.1 0.7 iota_compare_fusion.2
  68.8 0.6 iota_compare_fusion.1
  69.5 1.2 multiply_cosine_fusion.1
  70.7 23.6 %all-gather.2.cloned.1.call-done = bf16[256,2048]{1,0:T(8,128)(2,1)} async-done(((bf16[256,512]{1,0:T(8,128)(2,1)}), bf16[256,2048]{1,0:T(8,128)(2,1)}) %all-gather.2.cloned.1.call-update) | async-done | bytes 1048592 | tf_op jit(solution)/shard_map/all_gather | solution.py:122
  94.3 1.5 fusion.12
  95.8 3.5 fusion.84
  99.4 2.2 reshape.266
  101.6 1.9 multiply_reduce_fusion.3
  103.7 0.6 fusion.55
  105.7 0.9 fusion.54
  106.6 1.0 reshape.268
  107.6 1.0 collective-permute-done.1
  108.6 1.6 broadcast_select_fusion.3
  110.2 2.1 fusion.90
  112.3 1.5 fusion.88
  113.8 314.6 %all-to-all-done = bf16[64,2,128,512]{3,2,1,0:T(8,128)(2,1)} async-done(((bf16[64,2,128,512]{3,2,1,0:T(8,128)(2,1)}), bf16[64,2,128,512]{3,2,1,0:T(8,128)(2,1)}, u32[]{:S(2)}, u32[]{:S(2)}) %all-to-all-start) | async-done | bytes 16777248 | tf_op jit(solution)/shard_map/all_to_all | solution.py:145
  428.4 8.5 %copy.26 = bf16[1,2,64,128,512]{4,3,2,1,0:T(8,128)(2,1)S(1)} copy(bf16[1,2,64,128,512]{4,3,1,2,0:T(8,128)(2,1)} %bitcast.5) | data formatting | bytes 33554432 | tf_op jit(solution)/shard_map/all_to_all | solution.py:145
  436.8 1.4 fusion.89
  438.3 1.3 fusion
  439.6 1.3 fusion.6
  441.0 1.4 fusion.87
  442.4 1.3 fusion.2
  443.8 2.0 fusion.4
  445.8 0.9 fusion.19
  446.7 1.0 convert_element_type.79
  447.7 1.8 fusion.20
  449.5 1.0 convert_element_type.83
  450.5 1.7 convolution_convert_fusion
  452.2 0.8 dynamic-slice.1
  453.0 3.9 multiply_reduce_fusion.1
  456.9 53.3 %all-reduce.2.cloned.1.call-done = bf16[256,2048]{1,0:T(8,128)(2,1)} async-done(((bf16[256,2048]{1,0:T(8,128)(2,1)}), bf16[256,2048]{1,0:T(8,128)(2,1)}) %all-reduce.2.cloned.1.call-update) | async-done | bytes 1048592 | tf_op jit(solution)/shard_map/psum | solution.py:165
  510.2 1.5 fusion.10
  511.8 4.3 fusion.16
  516.0 4.9 multiply_reduce_fusion
  520.9 2.0 fusion.24
  (69 shorter events, 2.5 us)
Async XLA Ops:
  6.5 443.9 %copy-start = (bf16[512,2048]{1,0:T(8,128)(2,1)S(1)}, bf16[512,2048]{1,0:T(8,128)(2,1)}, u32[]{:S(2)}) copy-start(bf16[512,2048]{1,0:T(8,128)(2,1)} %param.25) | copy-start | bytes 6291460
  6.5 18.4 %collective-permute-start = (bf16[12,128,256]{2,1,0:T(8,128)(2,1)}, bf16[12,128,256]{2,1,0:T(8,128)(2,1)S(1)}, u32[]{:S(2)}, u32[]{:S(2)}) collective-permute-start(bf16[12,128,256]{2,1,0:T(8,128)(2,1)} %param.22), channel_id=1, source_target_pairs={{0,1},{1,0},{2,3},{3,2},{4,5},{5,4},{6,7},{7,6},{8,9},{9,8},{10,11... | collective-permute-start | bytes 2359304 | tf_op jit(solution)/shard_map/ppermute | solution.py:18
  51.2 15.4 %copy-start.17 = (s32[128,1]{0,1:T(1,128)S(1)}, s32[128,1]{0,1:T(1,128)}, u32[]{:S(2)}) copy-start(s32[128,1]{0,1:T(1,128)} %param.20) | copy-start | bytes 1540
  51.2 16.1 %copy-start.18 = (s32[12]{0:T(128)S(1)}, s32[12]{0:T(128)}, u32[]{:S(2)}) copy-start(s32[12]{0:T(128)} %param.21) | copy-start | bytes 148
  51.2 44.6 %copy-start.7 = (f32[2048]{0:T(1024)S(1)}, f32[2048]{0:T(1024)}, u32[]{:S(2)}) copy-start(f32[2048]{0:T(1024)} %param.26) | copy-start | bytes 24580
  51.2 377.1 %all-to-all-start = ((bf16[64,2,128,512]{3,2,1,0:T(8,128)(2,1)}), bf16[64,2,128,512]{3,2,1,0:T(8,128)(2,1)}, u32[]{:S(2)}, u32[]{:S(2)}) async-start(bf16[64,2,128,512]{3,2,1,0:T(8,128)(2,1)} %broadcast_select_fusion), calls=%async_computation | async-start | bytes 33554432 | tf_op jit(solution)/shard_map/all_to_all | solution.py:145
  65.9 28.4 %all-gather.2.cloned.1.call-start = ((), (), s32[]{:S(2)}) async-start(), calls=%async_computation.1 | async-start | bytes 1310720 | tf_op jit(solution)/shard_map/all_gather | solution.py:122
  66.6 443.6 %all-reduce.2.cloned.1.call-start = ((), (), s32[]{:S(2)}) async-start(), calls=%async_computation.2 | async-start | bytes 2097152 | tf_op jit(solution)/shard_map/psum | solution.py:165
  95.8 5.8 %copy-start.9 = (f32[256]{0:T(256)}, f32[256]{0:T(256)S(1)}, u32[]{:S(2)}) copy-start(f32[256]{0:T(256)S(1)} %add_rsqrt_fusion.5) | copy-start | bytes 3076
  95.8 5.7 %copy-start.1 = (bf16[256,2048]{1,0:T(8,128)(2,1)S(1)}, bf16[256,2048]{1,0:T(8,128)(2,1)}, u32[]{:S(2)}) copy-start(bf16[256,2048]{1,0:T(8,128)(2,1)} %all-gather.2.cloned.1.call-done) | copy-start | bytes 3145732
  99.4 4.2 copy-start.15
  101.6 3.0 copy-start.2
  101.6 3.4 copy-start.16
  103.5 1.8 copy-start.4
  104.3 4.3 collective-permute-start.1
  436.8 1.4 copy-start.14
  440.9 1.4 copy-start.13
  443.7 2.0 copy-start.3
  443.7 2.1 copy-start.6
  450.5 2.5 copy-start.8
  450.5 2.5 copy-start.10
  453.0 58.7 %copy-start.11 = (f32[2048]{0:T(1024)S(1)}, f32[2048]{0:T(1024)}, u32[]{:S(2)}) copy-start(f32[2048]{0:T(1024)} %param.32) | copy-start | bytes 24580
  453.0 58.7 %copy-start.12 = (f32[2048]{0:T(1024)S(1)}, f32[2048]{0:T(1024)}, u32[]{:S(2)}) copy-start(f32[2048]{0:T(1024)} %param.29) | copy-start | bytes 24580
  511.8 4.3 copy-start.5
Sparse Core Ops, SparseCore 0:
  68.5 25.7 all-gather.1
  452.4 57.8 all-reduce.1
where the time goes:
time: 531 us; the launch traced here: 530 us
  waiting for transfers between devices  407 us (77%)
  other arithmetic  37.8 us (7%)
  matrix products  28.4 us (5%)
  local copies, waits for them, and re-layouts  26.3 us (5%)
  starting transfers between devices  17 us (3%)
  between operations  13.8 us (3%)
    all_to_all x1, waiting for transfers between devices, shards(): lax.all_to_all(outgoing, 'seq', split_axis=0, concat_axis=2, tiled=True)[0]  315 us
    psum x1, waiting for transfers between devices, shards(): lax.psum(partial_out.astype(jnp.bfloat16), 'head').astype(jnp.float32)  53.3 us
    all_gather x1, waiting for transfers between devices, shards(): gathered = lax.all_gather(hidden_in, 'head', axis=1, tiled=True)  23.6 us
    all_to_all x1, starting transfers between devices, shards(): lax.all_to_all(outgoing, 'seq', split_axis=0, concat_axis=2, tiled=True)[0]  14.6 us
    ppermute x2, waiting for transfers between devices, partner(): return lax.ppermute(value, axis, pairs)  14.4 us
    select_n x2, other arithmetic, shards(): outgoing = jnp.take(paired, dest_groups, axis=0)  14.2 us
  transfers between devices with their start and end apart: 5, of which 5 were waited for; matrix products, arithmetic and copies ran while one was open for 6% of the time, Pallas kernels for 0%

commit v1 on v0

v1 whole, which is shorter than its diff:
```python
import functools
import math

import jax
import jax.numpy as jnp
import numpy as np
from jax import lax
from jax.experimental import pallas as pl
from jax.experimental.pallas import tpu as pltpu
from jax.sharding import PartitionSpec as P

MESH = pl.DeviceIdType.MESH
BF16 = jnp.bfloat16
F32 = jnp.float32

NEW = 128
NZ, NY, NC, NX = 8, 4, 2, 4
GROUPS = 12
BLOCK = 128
WIDTH = 2048
SHARE = WIDTH // NX
HEAD = 256
HALF = HEAD // 2
ROWS = 2 * NEW
OWN = ROWS // NX
SPAN = NY * NC * BLOCK
EPSILON = 1e-06
THETA = 1000000.0
LOW = -1e30


def place():
    s = lax.axis_index("seq")
    x = lax.axis_index("head")
    c = lax.rem(s, NC)
    y = lax.rem(lax.div(s, NC), NY)
    z = lax.div(s, NC * NY)
    return s, x, z, y, c


def seq_of(z, y, c):
    return (z * NY + y) * NC + c


def norm_rows(values):
    return values * lax.rsqrt(jnp.mean(values * values, axis=-1, keepdims=True) + EPSILON)


def greet(devices):
    barrier = pltpu.get_barrier_semaphore()
    for device in devices:
        pl.semaphore_signal(barrier, inc=1, device_id=device, device_id_type=MESH)
    pl.semaphore_wait(barrier, len(devices))


def send(src, dst, send_sem, recv_sem, device):
    copy = pltpu.make_async_remote_copy(
        src_ref=src,
        dst_ref=dst,
        send_sem=send_sem,
        recv_sem=recv_sem,
        device_id=device,
        device_id_type=MESH,
    )
    copy.start()
    return copy


def gather_kernel(
    groups_ref,
    lens_ref,
    inverse_ref,
    in_gain_ref,
    q_gain_ref,
    k_gain_ref,
    left_ref,
    right_ref,
    laurel_gain_ref,
    hidden_ref,
    cache_ref,
    wq_ref,
    wkv_ref,
    kv_ref,
    q_ref,
    fresh_ref,
    base_ref,
    meta_ref,
    hid,
    normed,
    wq,
    wkv,
    own_cache,
    own_q,
    own_fresh,
    local_sem,
    h_send,
    h_recv,
    c_send,
    c_recv,
    b_send,
    b_recv,
    q_send,
    q_recv,
    f_send,
    f_recv,
):
    s, x, z, y, c = place()
    part = lax.rem(x, 2)
    other = 1 - part
    up_y, down_y = lax.rem(y + 1, NY), lax.rem(y + NY - 1, NY)
    far_y = lax.rem(y + 2, NY)
    up_z, down_z = lax.rem(z + 1, NZ), lax.rem(z + NZ - 1, NZ)
    x_mate = x + 1 - 2 * part
    dev_yu, dev_yd = (seq_of(z, up_y, c), x), (seq_of(z, down_y, c), x)
    dev_zu, dev_zd = (seq_of(up_z, y, c), x), (seq_of(down_z, y, c), x)
    dev_mate = (s, x_mate)
    dev_core = (seq_of(z, y, 1 - c), x)
    x_peers = [(s, lax.rem(x + step, NX)) for step in range(1, NX)]

    take_hidden = pltpu.make_async_copy(hidden_ref, hid.at[x], local_sem.at[0])
    take_wq = pltpu.make_async_copy(wq_ref, wq, local_sem.at[1])
    take_wkv = pltpu.make_async_copy(wkv_ref, wkv, local_sem.at[2])
    take_cache = pltpu.make_async_copy(cache_ref, own_cache, local_sem.at[3])
    for copy in (take_hidden, take_wq, take_wkv, take_cache):
        copy.start()

    greet(x_peers + [dev_yu, dev_yd, dev_zu, dev_zd, dev_core])

    hidden_copies = [
        send(hidden_ref, hid.at[x], h_send.at[step], h_recv.at[step], x_peers[step])
        for step in range(NX - 1)
    ]
    mine = kv_ref.at[part, y, c]
    cache_up = send(cache_ref, mine, c_send.at[0], c_recv.at[0], dev_yu)
    cache_down = send(cache_ref, mine, c_send.at[1], c_recv.at[1], dev_yd)
    cache_x = send(cache_ref, mine, c_send.at[2], c_recv.at[2], dev_mate)

    def to_core(index, which, row):
        ref = kv_ref.at[which, row, c]
        src = cache_ref if index == 0 else ref
        return send(src, ref, b_send.at[index], b_recv.at[index], dev_core)

    core_copies = [to_core(0, part, y)]
    take_cache.wait()
    put_cache = pltpu.make_async_copy(own_cache, mine, local_sem.at[3])
    put_cache.start()

    row = lax.broadcasted_iota(jnp.int32, (ROWS, HALF), 0)
    lens = [lens_ref[groups_ref[2 * s + r, 0]] for r in range(2)]
    first = jnp.where(row < NEW, lens[0], lens[1] - NEW)
    angles = (first + row).astype(F32) * inverse_ref[...]
    cosine, sine = jnp.cos(angles), jnp.sin(angles)
    for far in range(NZ):
        for r in range(2):
            group = groups_ref[2 * seq_of(far, y, c) + r, 0]
            meta_ref[0, 2 * far + r] = group
            meta_ref[1, 2 * far + r] = lens_ref[group]

    def rotate(values):
        front, back = values[:, :HALF], values[:, HALF:]
        return jnp.concatenate(
            [front * cosine - back * sine, back * cosine + front * sine], axis=1
        )

    take_hidden.wait()
    for copy in hidden_copies:
        copy.wait_recv()
    total = jnp.zeros((ROWS, 1), F32)
    for k in range(NX):
        block = hid[k].astype(F32)
        total = total + jnp.sum(block * block, axis=1, keepdims=True)
    scale = lax.rsqrt(total / WIDTH + EPSILON)
    for k in range(NX):
        gain = in_gain_ref[:, k * SHARE : (k + 1) * SHARE]
        normed[k] = (hid[k].astype(F32) * scale * gain).astype(BF16)
    take_wq.wait()
    for head in range(2):
        value = jnp.zeros((ROWS, HEAD), F32)
        for k in range(NX):
            value = value + jnp.dot(
                normed[k],
                wq[k * SHARE : (k + 1) * SHARE, head * HEAD : (head + 1) * HEAD],
                preferred_element_type=F32,
            )
        value = rotate(norm_rows(value) * q_gain_ref[...]).astype(BF16)
        for r in range(2):
            own_q[r, head] = value[r * NEW : (r + 1) * NEW]
    take_wkv.wait()
    value = jnp.zeros((ROWS, HEAD), F32)
    for k in range(NX):
        value = value + jnp.dot(
            normed[k], wkv[k * SHARE : (k + 1) * SHARE, :], preferred_element_type=F32
        )
    value = norm_rows(value)
    own_fresh[...] = jnp.where(part == 0, rotate(value * k_gain_ref[...]), value).astype(BF16)

    put_q = pltpu.make_async_copy(own_q, q_ref.at[z], local_sem.at[0])
    put_q.start()

    ups, downs = {}, {}

    def q_up(step, piece):
        origin = lax.rem(z + NZ - step, NZ)
        ref = q_ref.at[origin, piece]
        src = own_q.at[piece] if step == 0 else ref
        ups[step, piece] = send(
            src, ref, q_send.at[0, step, piece], q_recv.at[0, step, piece], dev_zu
        )

    def q_down(step, piece):
        origin = lax.rem(z + step, NZ)
        ref = q_ref.at[origin, piece]
        src = own_q.at[piece] if step == 0 else ref
        downs[step, piece] = send(
            src, ref, q_send.at[1, step, piece], q_recv.at[1, step, piece], dev_zd
        )

    q_up(0, 0)
    q_down(0, 1)
    q_up(0, 1)
    q_down(0, 0)
    fresh_copy = send(own_fresh, fresh_ref.at[part], f_send, f_recv, dev_mate)
    put_fresh = pltpu.make_async_copy(own_fresh, fresh_ref.at[part], local_sem.at[1])
    put_fresh.start()

    def q_pass(step):
        ups[step - 1, 0].wait_recv()
        q_up(step, 0)
        downs[step - 1, 1].wait_recv()
        q_down(step, 1)
        ups[step - 1, 1].wait_recv()
        if step < 3:
            q_up(step, 1)
        downs[step - 1, 0].wait_recv()
        if step < 3:
            q_down(step, 0)

    half = GROUPS // 2
    cache_up.wait_recv()
    low = kv_ref.at[part, down_y, c, pl.ds(0, half)]
    far_up = send(low, low, c_send.at[3], c_recv.at[3], dev_yu)
    core_copies.append(to_core(1, part, down_y))
    cache_down.wait_recv()
    high = kv_ref.at[part, up_y, c, pl.ds(half, half)]
    far_down = send(high, high, c_send.at[4], c_recv.at[4], dev_yd)
    core_copies.append(to_core(2, part, up_y))
    cache_x.wait_recv()
    second = kv_ref.at[other, y, c]
    other_up = send(second, second, c_send.at[5], c_recv.at[5], dev_yu)
    other_down = send(second, second, c_send.at[6], c_recv.at[6], dev_yd)
    core_copies.append(to_core(3, other, y))
    q_pass(1)
    far_up.wait_recv()
    far_down.wait_recv()
    distant = kv_ref.at[part, far_y, c]
    far_x = send(distant, distant, c_send.at[7], c_recv.at[7], dev_mate)
    core_copies.append(to_core(4, part, far_y))
    q_pass(2)

    own_rows = pl.ds(pl.multiple_of(x * OWN, OWN), OWN)
    low_rank = jnp.zeros((OWN, left_ref.shape[1]), F32)
    for k in range(NX):
        low_rank = low_rank + jnp.dot(
            normed[k, own_rows, :],
            left_ref[k * SHARE : (k + 1) * SHARE, :],
            preferred_element_type=F32,
        )
    laurel = jnp.dot(low_rank.astype(BF16), right_ref[...], preferred_element_type=F32)
    laurel = norm_rows(laurel) * laurel_gain_ref[...]
    for k in range(NX):
        cols = slice(k * SHARE, (k + 1) * SHARE)
        base_ref[:, cols] = (
            hid[k, own_rows, :].astype(F32)
            + normed[k, own_rows, :].astype(F32)
            + laurel[:, cols]
        )

    q_pass(3)
    other_up.wait_recv()
    core_copies.append(to_core(5, other, down_y))
    other_down.wait_recv()
    core_copies.append(to_core(6, other, up_y))
    far_x.wait_recv()
    core_copies.append(to_core(7, other, far_y))
    ups[3, 0].wait_recv()
    downs[3, 1].wait_recv()
    fresh_copy.wait_recv()
    for copy in core_copies:
        copy.wait_recv()
    put_cache.wait()
    put_q.wait()
    put_fresh.wait()
    for copy in hidden_copies + core_copies + [
        cache_up,
        cache_down,
        cache_x,
        far_up,
        far_down,
        other_up,
        other_down,
        far_x,
        fresh_copy,
    ]:
        copy.wait_send()
    for copy in list(ups.values()) + list(downs.values()):
        copy.wait_send()


def attend_kernel(meta_ref, q_ref, k_ref, v_ref, fresh_ref, out_ref, lse_ref, m_sc, l_sc, acc):
    i = pl.program_id(0)
    s, x, z, y, c = place()
    live = meta_ref[1, i] - z * SPAN
    rows = q_ref[...].reshape(ROWS, HEAD)

    @pl.when(live <= 0)
    def _():
        m_sc[...] = jnp.full_like(m_sc, LOW)
        l_sc[...] = jnp.zeros_like(l_sc)
        acc[...] = jnp.zeros_like(acc)

    @pl.when(live > 0)
    def _():
        keys = k_ref[...].reshape(SPAN, HEAD)
        values = v_ref[...].reshape(SPAN, HEAD)
        scores = lax.dot_general(
            rows, keys, (((1,), (1,)), ((), ())), preferred_element_type=F32
        )
        slot = lax.broadcasted_iota(jnp.int32, (1, SPAN), 1)
        scores = jnp.where(slot < live, scores, LOW)
        top = jnp.max(scores, axis=1, keepdims=True)
        weights = jnp.exp(scores - top)
        m_sc[...] = jnp.broadcast_to(top, m_sc.shape)
        l_sc[...] = jnp.broadcast_to(jnp.sum(weights, axis=1, keepdims=True), l_sc.shape)
        acc[...] = jnp.dot(weights.astype(BF16), values, preferred_element_type=F32)

    @pl.when(lax.div(i, 2) == z)
    def _():
        mine = pl.ds(pl.multiple_of(lax.rem(i, 2) * NEW, NEW), NEW)
        scores = lax.dot_general(
            rows, fresh_ref[0, mine, :], (((1,), (1,)), ((), ())), preferred_element_type=F32
        )
        token = lax.rem(lax.broadcasted_iota(jnp.int32, (ROWS, NEW), 0), NEW)
        slot = lax.broadcasted_iota(jnp.int32, (ROWS, NEW), 1)
        scores = jnp.where(slot <= token, scores, LOW)
        before = m_sc[:, :1]
        top = jnp.maximum(before, jnp.max(scores, axis=1, keepdims=True))
        weights = jnp.exp(scores - top)
        keep = jnp.exp(before - top)
        m_sc[...] = jnp.broadcast_to(top, m_sc.shape)
        l_sc[...] = l_sc[...] * keep + jnp.sum(weights, axis=1, keepdims=True)
        acc[...] = acc[...] * keep + jnp.dot(
            weights.astype(BF16), fresh_ref[1, mine, :], preferred_element_type=F32
        )

    some = l_sc[...] > 0
    amount = jnp.where(some, l_sc[...], 1.0)
    out_ref[0] = (acc[...] / amount[:, :1]).astype(BF16)
    lse = jnp.where(some, m_sc[...] + jnp.log(amount), LOW)
    lse_ref[0] = jnp.transpose(lse)[:8]


def merge(first, second):
    rows_a, lse_a = first
    rows_b, lse_b = second
    top = jnp.maximum(lse_a, lse_b)
    wa, wb = jnp.exp(lse_a - top), jnp.exp(lse_b - top)
    total = wa + wb
    return rows_a * (wa / total) + rows_b * (wb / total), top + jnp.log(total)


def finish_kernel(
    part_ref,
    lse_ref,
    base_ref,
    ple_ref,
    post_gain_ref,
    ple_gain_ref,
    wout_ref,
    wgate_ref,
    wproj_ref,
    out_ref,
    part,
    wout,
    wgate,
    wproj,
    o_out,
    l_out,
    o_in,
    l_in,
    p_out,
    p_in,
    res,
    local_sem,
    o_send,
    o_recv,
    l_send,
    l_recv,
    p_send,
    p_recv,
    r_send,
    r_recv,
):
    s, x, z, y, c = place()
    up_z, down_z = lax.rem(z + 1, NZ), lax.rem(z + NZ - 1, NZ)
    dev_zu, dev_zd = (seq_of(up_z, y, c), x), (seq_of(down_z, y, c), x)
    x_peers = [(s, lax.rem(x + step, NX)) for step in range(1, NX)]

    take_part = pltpu.make_async_copy(part_ref, part, local_sem.at[0])
    take_wout = pltpu.make_async_copy(wout_ref, wout, local_sem.at[1])
    take_wgate = pltpu.make_async_copy(wgate_ref, wgate, local_sem.at[2])
    take_wproj = pltpu.make_async_copy(wproj_ref, wproj, local_sem.at[3])
    for copy in (take_part, take_wout, take_wgate, take_wproj):
        copy.start()
    greet(x_peers + [dev_zu, dev_zd])
    take_part.wait()

    def column(block):
        return jnp.transpose(block)[:, :1]

    copies = {}
    reach = {(0, 0): 4, (0, 1): 3, (1, 0): 3, (1, 1): 4}

    def target(way, r, step):
        distance = reach[way, r] - step
        return lax.rem(z + distance, NZ) if way == 0 else lax.rem(z + NZ - distance, NZ)

    def mine(index):
        return part[index].astype(F32), column(lse_ref[index])

    def arrived(way, r, step):
        o_copy, l_copy = copies[way, r, step]
        o_copy.wait_recv()
        l_copy.wait_recv()
        return o_in[way, r, step].astype(F32), column(l_in[way, r, step])

    def hop(way, r, step):
        index = 2 * target(way, r, step) + r
        if step == 0:
            o_src, l_src = part.at[index], lse_ref.at[index]
        else:
            rows, lse = merge(mine(index), arrived(way, r, step - 1))
            o_out[way, r, step] = rows.astype(BF16)
            l_out[way, r, step] = jnp.transpose(jnp.broadcast_to(lse, (ROWS, 128)))[:8]
            o_src, l_src = o_out.at[way, r, step], l_out.at[way, r, step]
        device = dev_zu if way == 0 else dev_zd
        copies[way, r, step] = (
            send(
                o_src,
                o_in.at[way, r, step],
                o_send.at[way, r, step],
                o_recv.at[way, r, step],
                device,
            ),
            send(
                l_src,
                l_in.at[way, r, step],
                l_send.at[way, r, step],
                l_recv.at[way, r, step],
                device,
            ),
        )

    for step in range(4):
        for way, r in ((0, 0), (1, 1), (1, 0), (0, 1)):
            if step < reach[way, r]:
                hop(way, r, step)

    take_wout.wait()
    for r in range(2):
        value = mine(2 * z + r)
        value = merge(value, arrived(0, r, reach[0, r] - 1))
        value = merge(value, arrived(1, r, reach[1, r] - 1))
        rows = value[0].astype(BF16)
        total = jnp.dot(rows[:NEW], wout[:HEAD], preferred_element_type=F32)
        total = total + jnp.dot(rows[NEW:], wout[HEAD:], preferred_element_type=F32)
        total = total.astype(BF16)
        p_out[2 * r] = total[:OWN]
        p_out[2 * r + 1] = total[OWN:]

    p_copies = [
        send(
            p_out.at[x_peers[step][1]],
            p_in.at[step],
            p_send.at[step],
            p_recv.at[step],
            x_peers[step],
        )
        for step in range(NX - 1)
    ]
    take_wgate.wait()
    take_wproj.wait()
    projected = p_out[x].astype(F32)
    for step in range(NX - 1):
        p_copies[step].wait_recv()
        projected = projected + p_in[step].astype(F32)
    combined = (base_ref[...] + norm_rows(projected) * post_gain_ref[...]) * math.sqrt(0.5)
    gate_in = jnp.dot(combined.astype(BF16), wgate[...], preferred_element_type=F32)
    own_rows = pl.ds(pl.multiple_of(x * OWN, OWN), OWN)
    gated = jax.nn.gelu(gate_in, approximate=True) * ple_ref[own_rows, :].astype(F32)
    ple_out = jnp.dot(gated.astype(BF16), wproj[...], preferred_element_type=F32)
    result = (combined + norm_rows(ple_out) * ple_gain_ref[...]).astype(BF16)
    for k in range(NX):
        res[k] = result[:, k * SHARE : (k + 1) * SHARE]
    r_copies = [
        send(
            res.at[x_peers[step][1]],
            out_ref.at[own_rows],
            r_send.at[step],
            r_recv.at[step],
            x_peers[step],
        )
        for step in range(NX - 1)
    ]
    out_ref[own_rows, :] = res[x]
    for copy in r_copies:
        copy.wait_recv()
    for copy in p_copies + r_copies:
        copy.wait_send()
    for o_copy, l_copy in copies.values():
        o_copy.wait_send()
        l_copy.wait_send()


def any_spec():
    return pl.BlockSpec(memory_space=pl.ANY)


def vmem_spec():
    return pl.BlockSpec(memory_space=pltpu.VMEM)


def smem_spec():
    return pl.BlockSpec(memory_space=pltpu.SMEM)


def shards(
    hidden_in,
    ple_in,
    group_map,
    prompt_len,
    cache,
    w_query,
    key_value_weight,
    w_out,
    in_gain,
    q_gain,
    k_gain,
    post_gain,
    laurel_left,
    laurel_right,
    laurel_gain,
    w_plgate,
    w_plproj,
    ple_gain,
):
    inverse = np.power(THETA, -np.arange(HALF) / HALF).astype(np.float32)[None, :]
    dma = pltpu.SemaphoreType.DMA
    kv, queries, fresh, base, meta = pl.pallas_call(
        gather_kernel,
        name="gather_kernel",
        out_shape=(
            jax.ShapeDtypeStruct((2, NY, NC, GROUPS, BLOCK, HEAD), BF16),
            jax.ShapeDtypeStruct((NZ, 2, 2, NEW, HEAD), BF16),
            jax.ShapeDtypeStruct((2, ROWS, HEAD), BF16),
            jax.ShapeDtypeStruct((OWN, WIDTH), F32),
            jax.ShapeDtypeStruct((2, 2 * NZ), jnp.int32),
        ),
        in_specs=[smem_spec()] * 2 + [vmem_spec()] * 7 + [any_spec()] * 4,
        out_specs=(any_spec(), any_spec(), any_spec(), vmem_spec(), smem_spec()),
        scratch_shapes=[
            pltpu.VMEM((NX, ROWS, SHARE), BF16),
            pltpu.VMEM((NX, ROWS, SHARE), BF16),
            pltpu.VMEM((WIDTH, 2 * HEAD), BF16),
            pltpu.VMEM((WIDTH, HEAD), BF16),
            pltpu.VMEM((GROUPS, BLOCK, HEAD), BF16),
            pltpu.VMEM((2, 2, NEW, HEAD), BF16),
            pltpu.VMEM((ROWS, HEAD), BF16),
            dma((4,)),
            dma((3,)),
            dma((3,)),
            dma((8,)),
            dma((8,)),
            dma((8,)),
            dma((8,)),
            dma((2, 4, 2)),
            dma((2, 4, 2)),
            dma,
            dma,
        ],
        compiler_params=pltpu.CompilerParams(collective_id=0, has_side_effects=True),
    )(
        group_map,
        prompt_len,
        jnp.asarray(inverse),
        in_gain[None, :],
        q_gain[None, :],
        k_gain[None, :],
        laurel_left,
        laurel_right,
        laurel_gain[None, :],
        hidden_in,
        cache,
        w_query,
        key_value_weight,
    )
    requests = 2 * NZ
    part, lse = pl.pallas_call(
        attend_kernel,
        name="attend_kernel",
        out_shape=(
            jax.ShapeDtypeStruct((requests, ROWS, HEAD), BF16),
            jax.ShapeDtypeStruct((requests, 8, ROWS), F32),
        ),
        grid_spec=pltpu.PrefetchScalarGridSpec(
            num_scalar_prefetch=1,
            grid=(requests,),
            in_specs=[
                pl.BlockSpec(
                    (1, 1, 2, NEW, HEAD), lambda i, m: (lax.div(i, 2), lax.rem(i, 2), 0, 0, 0)
                ),
                pl.BlockSpec((1, NY, NC, 1, BLOCK, HEAD), lambda i, m: (0, 0, 0, m[0, i], 0, 0)),
                pl.BlockSpec((1, NY, NC, 1, BLOCK, HEAD), lambda i, m: (1, 0, 0, m[0, i], 0, 0)),
                pl.BlockSpec((2, ROWS, HEAD), lambda i, m: (0, 0, 0)),
            ],
            out_specs=[
                pl.BlockSpec((1, ROWS, HEAD), lambda i, m: (i, 0, 0)),
                pl.BlockSpec((1, 8, ROWS), lambda i, m: (i, 0, 0)),
            ],
            scratch_shapes=[
                pltpu.VMEM((ROWS, 128), F32),
                pltpu.VMEM((ROWS, 128), F32),
                pltpu.VMEM((ROWS, HEAD), F32),
            ],
        ),
        compiler_params=pltpu.CompilerParams(dimension_semantics=("arbitrary",)),
    )(meta, queries, kv, kv, fresh)
    hops = (2, 2, 4)
    return pl.pallas_call(
        finish_kernel,
        name="finish_kernel",
        out_shape=jax.ShapeDtypeStruct((ROWS, SHARE), BF16),
        in_specs=[any_spec()] + [vmem_spec()] * 5 + [any_spec()] * 3,
        out_specs=vmem_spec(),
        scratch_shapes=[
            pltpu.VMEM((requests, ROWS, HEAD), BF16),
            pltpu.VMEM((2 * HEAD, WIDTH), BF16),
            pltpu.VMEM((WIDTH, HEAD), BF16),
            pltpu.VMEM((HEAD, WIDTH), BF16),
            pltpu.VMEM(hops + (ROWS, HEAD), BF16),
            pltpu.VMEM(hops + (8, ROWS), F32),
            pltpu.VMEM(hops + (ROWS, HEAD), BF16),
            pltpu.VMEM(hops + (8, ROWS), F32),
            pltpu.VMEM((NX, OWN, WIDTH), BF16),
            pltpu.VMEM((NX - 1, OWN, WIDTH), BF16),
            pltpu.VMEM((NX, OWN, SHARE), BF16),
            dma((4,)),
            dma(hops),
            dma(hops),
            dma(hops),
            dma(hops),
            dma((3,)),
            dma((3,)),
            dma((3,)),
            dma((3,)),
        ],
        compiler_params=pltpu.CompilerParams(collective_id=1, has_side_effects=True),
    )(
        part,
        lse,
        base,
        ple_in,
        post_gain[None, :],
        ple_gain[None, :],
        w_out,
        w_plgate,
        w_plproj,
    )


def solution(mesh):
    placed = (
        P("seq", "head"),
        P("seq", None),
        P(),
        P(),
        P(None, "seq", "head"),
        P(None, "head"),
        P(None, "head"),
        P("head", None),
        P(),
        P(),
        P(),
        P(),
        P(),
        P(),
        P(),
        P(),
        P(),
        P(),
    )
    return jax.shard_map(
        shards, mesh=mesh, in_specs=placed, out_specs=P("seq", "head"), check_vma=False
    )
```

time: 531 us -> 141 us (0.27)
  waiting for transfers between devices: 407 us -> 0 us
  Pallas kernels: 0 us -> 136 us
  other arithmetic: 37.8 us -> 0 us
  matrix products: 28.4 us -> 0 us
  local copies, waits for them, and re-layouts: 26.3 us -> 5.04 us
  starting transfers between devices: 17 us -> 0 us
  between operations: 13.8 us -> 0.02 us
    all_to_all x1 -> x0, waiting for transfers between devices: 315 us -> none  [shards(): lax.all_to_all(outgoing, 'seq', split_axis=0, concat_axis=2, tiled=True)[0]]
    pallas_call x0 -> x3, Pallas kernels: none -> 136 us  [the longest x1 65.6 us: shards(): pl.pallas_call(gather_kernel, name='gather_kernel', out_shape=(jax.ShapeD...]
    psum x1 -> x0, waiting for transfers between devices: 53.3 us -> none  [shards(): lax.psum(partial_out.astype(jnp.bfloat16), 'head').astype(jnp.float32)]
    dot_general x13 -> x0, matrix products: 28.4 us -> none  [the longest x4 6.43 us: contract_last(): lax.dot_general(left_rows, right_rows, (((1,), (1,)), ((), ())), preferre...]
    all_gather x1 -> x0, waiting for transfers between devices: 23.6 us -> none  [shards(): gathered = lax.all_gather(hidden_in, 'head', axis=1, tiled=True)]
    select_n x5 -> x0, other arithmetic: 17.6 us -> none  [the longest x2 14.2 us: shards(): outgoing = jnp.take(paired, dest_groups, axis=0)]
    all_to_all x1 -> x0, starting transfers between devices: 14.6 us -> none  [shards(): lax.all_to_all(outgoing, 'seq', split_axis=0, concat_axis=2, tiled=True)[0]]
    ppermute x2 -> x0, waiting for transfers between devices: 14.4 us -> none  [partner(): return lax.ppermute(value, axis, pairs)]
  transfers between devices with their start and end apart: 5 -> 0, of which waited for: 5 -> 0; matrix products, arithmetic and copies ran while one was open for 6% -> 0% of each run, Pallas kernels for 0% -> 0%
where the time goes in v1:
time: 141 us
  Pallas kernels  136 us (96%)
  local copies, waits for them, and re-layouts  5.04 us (4%)
    pallas_call x1, Pallas kernels, shards(): pl.pallas_call(gather_kernel, name='gather_kernel', out_shape=(jax.ShapeD...  65.6 us
    pallas_call x1, Pallas kernels, shards(): pl.pallas_call(finish_kernel, name='finish_kernel', out_shape=jax.ShapeDt...  47.3 us
    pallas_call x1, Pallas kernels, shards(): pl.pallas_call(attend_kernel, name='attend_kernel', out_shape=(jax.ShapeD...  22.6 us
    unnamed x3, local copies, waits for them, and re-layouts  5.04 us

profile of v1, /device:TPU:1, one launch (start us, length us, event | category | flops | bytes accessed | tf_op | source)
XLA Modules:
  0.0 140.6 jit_solution(11637943519602596769)
XLA Ops:
  0.0 1.4 copy.20.groups_ref
  1.4 2.0 %copy.21.left_ref = bf16[2048,64]{1,0:T(8,128)(2,1)} copy(bf16[2048,64]{0,1:T(8,128)(2,1)} %param.31) | data formatting | bytes 524288 | tf_op args[12]
  3.4 65.6 %gather_kernel.1 = (bf16[2,4,2,12,128,256]{5,4,3,2,1,0:T(8,128)(2,1)}, bf16[8,2,2,128,256]{4,3,2,1,0:T(8,128)(2,1)}, bf16[2,256,256]{2,1,0:T(8,128)(2,1)}, f32[64,2048]{1,0:T(8,128)}, s32[2,16]{1,0:T(2,128)}) custom-call(s32[128,1]{1,0:T(8,128)} %copy.20.groups_ref, s32[12]{0:T(128)} %lens_ref.1, f32[1,128]{1,0:T(1,128)} %constant.2.clone.inverse_ref, ...), custom_call_target="tpu_custom_call" | custom-call | tf_op jit(solution)/shard_map/gather_kernel/pallas_call | solution.py:558
  69.0 22.6 %attend_kernel.1 = (bf16[16,256,256]{2,1,0:T(8,128)(2,1)}, f32[16,8,256]{2,1,0:T(8,128)}) custom-call(s32[2,16]{1,0:T(2,128)} %get-tuple-element.12.meta_ref, bf16[8,2,2,128,256]{4,3,2,1,0:T(8,128)(2,1)} %get-tuple-element.13.q_ref, bf16[2,4,2,12,128,256]{5,4,3,2,1,0:T(8,128)(2,1)} %get-tuple-element.14.k_ref.v_ref, ...), custom_call_target="tpu_custom_call" | custom-call | tf_op jit(solution)/shard_map/attend_kernel/pallas_call | solution.py:607
  91.7 47.3 %finish_kernel.1 = bf16[256,512]{1,0:T(8,128)(2,1)} custom-call(bf16[16,256,256]{2,1,0:T(8,128)(2,1)} %get-tuple-element.16.part_ref, f32[16,8,256]{2,1,0:T(8,128)} %get-tuple-element.17.lse_ref, f32[64,2048]{1,0:T(8,128)} %get-tuple-element.18.base_ref, bf16[256,256]{1,0:T(8,128)(2,1)} %ple_ref.1, f32[1,2048]{1,0:T(1,128)} %bitcast.8, f32[1,2048]{1,0:T(1,128)} %bitcast.9, ...), custom_call_target="tpu_custom_call" | custom-call | tf_op jit(solution)/shard_map/finish_kernel/pallas_call | solution.py:638
  139.0 1.7 %copy.23 = bf16[256,512]{1,0:T(8,128)(2,1)} copy(bf16[256,512]{1,0:T(8,128)(2,1)} %finish_kernel.1) | data formatting | bytes 524288
